TPU v7x, 256 devices: a whole 4x4x8 slice. The times are simulated.
256 devices in a mesh: wide: 32 (over z, x), narrow: 8 (over y, core).
Axes of the slice: x: 4, y: 4, z: 8, core: 2. Of those that a mesh axis runs over, the one named last changes fastest.
Arguments:
- cube: bfloat16 [256, 1536, 224], P('narrow', 'wide')
Outputs:
- restored: bfloat16 [256, 1536, 224], P('narrow', 'wide')
- projector: float32 [224, 224], replicated
All inputs are finite; a program needn't handle non-finite values.
Results may differ from a plain program's by a relative error of at most 0.0034.
Values may be sent and summed in bfloat16 or wider, within the bound.
A program may use at most 64 MiB of HBM per device.

v0:
```python
import jax
import jax.numpy as jnp
from jax import lax
from jax.sharding import PartitionSpec as P

TILE_ROWS = 32
TILE_COLS = 48
BANDS = 224
RANK = 16
POWER_ITERS = 4
TV_ITERS = 3
hi_prec = lax.Precision.HIGHEST


def with_halo(cells, sides, width):
    for axis, dim in sides:
        count = lax.axis_size(axis)
        ends = count - 1
        head = lax.slice_in_dim(cells, 0, width, axis=dim)
        tail = lax.slice_in_dim(cells, cells.shape[dim] - width, cells.shape[dim], axis=dim)
        cells = jnp.concatenate(
            [
                lax.ppermute(tail, axis, [(i, (i + 1) % count) for i in range(ends)]),
                cells,
                lax.ppermute(head, axis, [((i + 1) % count, i) for i in range(ends)]),
            ],
            axis=dim,
        )
    return cells


def smooth_step(field, fitted, grow, gcol, height, width):
    mask_x = ((grow >= 0) & (grow + 1 < height)).astype(jnp.float32)
    mask_y = ((gcol >= 0) & (gcol + 1 < width)).astype(jnp.float32)
    corner = field[:-1, :-1]
    grad_x = (field[1:, :-1] - corner) * mask_x[:-1, None, None]
    grad_y = (field[:-1, 1:] - corner) * mask_y[None, :-1, None]
    magnitude = jnp.sqrt(grad_x * grad_x + grad_y * grad_y + 0.25)
    flow_x = grad_x / magnitude
    flow_y = grad_y / magnitude
    diverg = flow_x[1:, 1:] - flow_x[:-1, 1:] + flow_y[1:, 1:] - flow_y[1:, :-1]
    centre = field[1:-1, 1:-1]
    return centre - 0.5 * (centre - fitted[1:-1, 1:-1] - 0.5 * diverg)


def subspace(gram):
    bands = lax.broadcasted_iota(jnp.float32, (BANDS, RANK), 0)
    cols = lax.broadcasted_iota(jnp.float32, (BANDS, RANK), 1)
    basis = jnp.cos(jnp.pi * (bands + 0.5) * cols / BANDS)
    for step in range(POWER_ITERS):
        grown = jnp.dot(gram, basis, precision=hi_prec)
        inner = jnp.dot(grown.T, grown, precision=hi_prec)
        lower = jnp.linalg.cholesky(inner)
        basis = jax.scipy.linalg.solve_triangular(lower, grown.T, lower=True).T
    return basis


def project_tile(block, basis, basis_low):
    loading = jnp.einsum("hwb,br->hwr", block, basis_low, preferred_element_type=jnp.float32)
    return jnp.einsum("hwr,br->hwb", loading, basis, precision=hi_prec)


def body(cube):
    n_rows = lax.axis_size("narrow")
    n_cols = lax.axis_size("wide")
    height = TILE_ROWS * n_rows
    width = TILE_COLS * n_cols
    row_base = lax.axis_index("narrow") * TILE_ROWS
    col_base = lax.axis_index("wide") * TILE_COLS
    flat = cube.reshape(TILE_ROWS * TILE_COLS, BANDS)
    local = lax.dot_general(
        flat, flat, (((0,), (0,)), ((), ())), preferred_element_type=jnp.float32
    )
    total = lax.psum(local, ("wide", "narrow"))
    gram = total / (height * width)
    basis = subspace(gram)
    projector = jnp.dot(basis, basis.T, precision=hi_prec)
    basis_low = basis.astype(jnp.bfloat16)
    fitted = project_tile(cube, basis, basis_low)
    fitted_pad = jnp.pad(fitted, ((1, 1), (1, 1), (0, 0)))
    rows = row_base - 1 + jnp.arange(TILE_ROWS + 2, dtype=jnp.int32)
    cols = col_base - 1 + jnp.arange(TILE_COLS + 2, dtype=jnp.int32)
    field = fitted
    for step in range(TV_ITERS):
        field_ext = with_halo(field, (("narrow", 0), ("wide", 1)), 1)
        field = smooth_step(field_ext, fitted_pad, rows, cols, height, width)
    return (field.astype(jnp.bfloat16), projector)


def solution(mesh):
    return jax.shard_map(
        body,
        mesh=mesh,
        in_specs=(P("narrow", "wide", None),),
        out_specs=(P("narrow", "wide", None), P()),
        check_vma=False,
    )
```

profile of v0, /device:TPU:111, one launch (start us, length us, event | category | flops | bytes accessed | tf_op | source)
XLA Modules:
  0.0 365.4 jit_solution(9770431130495249108)
XLA Ops:
  7.2 1.1 copy-done
  8.3 1.1 convolution_bitcast_fusion.1
  9.5 258.3 %all-reduce.2.cloned.1.call-done = f32[224,224]{1,0:T(8,128)} async-done(((f32[224,224]{1,0:T(8,128)}), f32[224,224]{1,0:T(8,128)}) %all-reduce.2.cloned.1.call-update) | async-done | bytes 200720 | tf_op jit(solution)/shard_map/psum | solution.py:74
  267.8 1.7 fusion.34
  269.7 1.5 cholesky.74
  271.2 0.6 compare_reduce_fusion.3
  271.9 0.6 fusion.56
  272.5 1.2 custom-call.8
  273.9 1.2 fusion.32
  275.4 1.5 cholesky.85
  276.9 0.6 compare_reduce_fusion.2
  277.6 0.6 fusion.57
  278.2 1.2 custom-call.9
  279.6 1.2 fusion.30
  281.1 1.5 cholesky.96
  283.3 0.6 fusion.58
  283.9 1.2 custom-call.10
  285.4 1.2 fusion.28
  286.8 1.5 cholesky.107
  288.3 0.6 compare_reduce_fusion
  289.0 0.6 fusion.59
  289.6 1.2 custom-call.11
  291.6 1.5 fusion.46
  293.1 1.9 collective-permute-start
  295.0 2.4 collective-permute-start.1
  297.4 3.0 collective-permute-done.1
  300.5 3.5 collective-permute-start.2
  304.0 1.9 collective-permute-start.3
  306.1 5.9 %collective-permute-done.3 = f32[34,1,224]{2,1,0:T(1,128)S(1)} collective-permute-done((f32[34,1,224]{2,1,0:T(1,128)S(1)}, f32[34,1,224]{2,1,0:T(1,128)S(1)}, u32[]{:S(2)}, u32[]{:S(2)}) %collective-permute-start.3) | collective-permute-done | bytes 30496 | tf_op jit(solution)/shard_map/ppermute | solution.py:25
  312.0 1.4 fusion.14
  313.4 0.7 fusion.27
  314.1 3.5 collective-permute-start.4
  317.6 1.9 collective-permute-start.5
  319.5 3.5 collective-permute-done.5
  323.0 1.9 collective-permute-start.6
  325.0 3.4 collective-permute-start.7
  328.6 4.4 %collective-permute-done.7 = f32[34,1,224]{2,1,0:T(1,128)S(1)} collective-permute-done((f32[34,1,224]{2,1,0:T(1,128)S(1)}, f32[34,1,224]{2,1,0:T(1,128)S(1)}, u32[]{:S(2)}, u32[]{:S(2)}) %collective-permute-start.7) | collective-permute-done | bytes 30496 | tf_op jit(solution)/shard_map/ppermute | solution.py:25
  333.0 1.4 fusion.12
  334.4 1.1 fusion.23
  335.5 3.1 collective-permute-start.8
  338.6 1.9 collective-permute-start.9
  340.5 3.5 collective-permute-done.9
  344.1 1.9 collective-permute-start.10
  346.0 1.1 fusion.88
  347.1 3.5 collective-permute-start.11
  350.8 4.2 %collective-permute-done.11 = f32[34,1,224]{2,1,0:T(1,128)S(1)} collective-permute-done((f32[34,1,224]{2,1,0:T(1,128)S(1)}, f32[34,1,224]{2,1,0:T(1,128)S(1)}, u32[]{:S(2)}, u32[]{:S(2)}) %collective-permute-start.11) | collective-permute-done | bytes 30496 | tf_op jit(solution)/shard_map/ppermute | solution.py:25
  355.1 1.4 fusion.10
  356.5 2.0 fusion.19
  (45 shorter events, 4.0 us)
Async XLA Ops:
  7.2 1.1 copy-start
  7.2 260.6 %all-reduce.2.cloned.1.call-start = ((), (), s32[]{:S(2)}) async-start(), calls=%async_computation | async-start | bytes 458752 | tf_op jit(solution)/shard_map/psum | solution.py:74
  293.1 4.4 %collective-permute-start = (f32[1,48,224]{2,1,0:T(8,128)S(1)}, f32[1,48,224]{2,1,0:T(8,128)S(1)}, u32[]{:S(2)}, u32[]{:S(2)}) collective-permute-start(f32[1,48,224]{2,1,0:T(8,128)S(1)} %get-tuple-element.20), channel_id=1, source_target_pairs={{0,1},{1,2},{2,3},{3,4},{4,5},{5,6},{6,7},{8,9},{9,10},{10,11},{11... | collective-permute-start | bytes 129032 | tf_op jit(solution)/shard_map/ppermute | solution.py:23
  295.0 5.4 %collective-permute-start.1 = (f32[1,48,224]{2,1,0:T(8,128)S(1)}, f32[1,48,224]{2,1,0:T(8,128)S(1)}, u32[]{:S(2)}, u32[]{:S(2)}) collective-permute-start(f32[1,48,224]{2,1,0:T(8,128)S(1)} %get-tuple-element.21), channel_id=1, source_target_pairs={{1,0},{2,1},{3,2},{4,3},{5,4},{6,5},{7,6},{9,8},{10,9},{11,10},{12... | collective-permute-start | bytes 129032 | tf_op jit(solution)/shard_map/ppermute | solution.py:25
  300.5 5.5 %collective-permute-start.2 = (f32[34,1,224]{2,1,0:T(1,128)S(1)}, f32[34,1,224]{2,1,0:T(1,128)S(1)}, u32[]{:S(2)}, u32[]{:S(2)}) collective-permute-start(f32[34,1,224]{2,1,0:T(1,128)S(1)} %get-tuple-element.15), channel_id=1, source_target_pairs={{0,8},{8,16},{16,24},{24,32},{32,40},{40,48},{48,56},{56,64},{64,7... | collective-permute-start | bytes 91400 | tf_op jit(solution)/shard_map/ppermute | solution.py:23
  304.0 8.0 %collective-permute-start.3 = (f32[34,1,224]{2,1,0:T(1,128)S(1)}, f32[34,1,224]{2,1,0:T(1,128)S(1)}, u32[]{:S(2)}, u32[]{:S(2)}) collective-permute-start(f32[34,1,224]{2,1,0:T(1,128)S(1)} %get-tuple-element.14), channel_id=1, source_target_pairs={{8,0},{16,8},{24,16},{32,24},{40,32},{48,40},{56,48},{64,56},{72,6... | collective-permute-start | bytes 91400 | tf_op jit(solution)/shard_map/ppermute | solution.py:25
  314.1 5.4 %collective-permute-start.4 = (f32[1,48,224]{2,1,0:T(8,128)S(1)}, f32[1,48,224]{2,1,0:T(8,128)S(1)}, u32[]{:S(2)}, u32[]{:S(2)}) collective-permute-start(f32[1,48,224]{2,1,0:T(8,128)S(1)} %get-tuple-element.18), channel_id=1, source_target_pairs={{0,1},{1,2},{2,3},{3,4},{4,5},{5,6},{6,7},{8,9},{9,10},{10,11},{11... | collective-permute-start | bytes 129032 | tf_op jit(solution)/shard_map/ppermute | solution.py:23
  317.6 5.4 %collective-permute-start.5 = (f32[1,48,224]{2,1,0:T(8,128)S(1)}, f32[1,48,224]{2,1,0:T(8,128)S(1)}, u32[]{:S(2)}, u32[]{:S(2)}) collective-permute-start(f32[1,48,224]{2,1,0:T(8,128)S(1)} %get-tuple-element.19), channel_id=1, source_target_pairs={{1,0},{2,1},{3,2},{4,3},{5,4},{6,5},{7,6},{9,8},{10,9},{11,10},{12... | collective-permute-start | bytes 129032 | tf_op jit(solution)/shard_map/ppermute | solution.py:25
  323.0 5.3 %collective-permute-start.6 = (f32[34,1,224]{2,1,0:T(1,128)S(1)}, f32[34,1,224]{2,1,0:T(1,128)S(1)}, u32[]{:S(2)}, u32[]{:S(2)}) collective-permute-start(f32[34,1,224]{2,1,0:T(1,128)S(1)} %get-tuple-element.13), channel_id=1, source_target_pairs={{0,8},{8,16},{16,24},{24,32},{32,40},{40,48},{48,56},{56,64},{64,7... | collective-permute-start | bytes 91400 | tf_op jit(solution)/shard_map/ppermute | solution.py:23
  325.0 8.0 %collective-permute-start.7 = (f32[34,1,224]{2,1,0:T(1,128)S(1)}, f32[34,1,224]{2,1,0:T(1,128)S(1)}, u32[]{:S(2)}, u32[]{:S(2)}) collective-permute-start(f32[34,1,224]{2,1,0:T(1,128)S(1)} %get-tuple-element.12), channel_id=1, source_target_pairs={{8,0},{16,8},{24,16},{32,24},{40,32},{48,40},{56,48},{64,56},{72,6... | collective-permute-start | bytes 91400 | tf_op jit(solution)/shard_map/ppermute | solution.py:25
  335.5 5.1 %collective-permute-start.8 = (f32[1,48,224]{2,1,0:T(8,128)S(1)}, f32[1,48,224]{2,1,0:T(8,128)S(1)}, u32[]{:S(2)}, u32[]{:S(2)}) collective-permute-start(f32[1,48,224]{2,1,0:T(8,128)S(1)} %get-tuple-element.16), channel_id=1, source_target_pairs={{0,1},{1,2},{2,3},{3,4},{4,5},{5,6},{6,7},{8,9},{9,10},{10,11},{11... | collective-permute-start | bytes 129032 | tf_op jit(solution)/shard_map/ppermute | solution.py:23
  338.6 5.4 %collective-permute-start.9 = (f32[1,48,224]{2,1,0:T(8,128)S(1)}, f32[1,48,224]{2,1,0:T(8,128)S(1)}, u32[]{:S(2)}, u32[]{:S(2)}) collective-permute-start(f32[1,48,224]{2,1,0:T(8,128)S(1)} %get-tuple-element.17), channel_id=1, source_target_pairs={{1,0},{2,1},{3,2},{4,3},{5,4},{6,5},{7,6},{9,8},{10,9},{11,10},{12... | collective-permute-start | bytes 129032 | tf_op jit(solution)/shard_map/ppermute | solution.py:25
  344.1 6.5 %collective-permute-start.10 = (f32[34,1,224]{2,1,0:T(1,128)S(1)}, f32[34,1,224]{2,1,0:T(1,128)S(1)}, u32[]{:S(2)}, u32[]{:S(2)}) collective-permute-start(f32[34,1,224]{2,1,0:T(1,128)S(1)} %get-tuple-element.11), channel_id=1, source_target_pairs={{0,8},{8,16},{16,24},{24,32},{32,40},{40,48},{48,56},{56,64},{64,7... | collective-permute-start | bytes 91400 | tf_op jit(solution)/shard_map/ppermute | solution.py:23
  347.1 8.0 %collective-permute-start.11 = (f32[34,1,224]{2,1,0:T(1,128)S(1)}, f32[34,1,224]{2,1,0:T(1,128)S(1)}, u32[]{:S(2)}, u32[]{:S(2)}) collective-permute-start(f32[34,1,224]{2,1,0:T(1,128)S(1)} %get-tuple-element.10), channel_id=1, source_target_pairs={{8,0},{16,8},{24,16},{32,24},{40,32},{48,40},{56,48},{64,56},{72,6... | collective-permute-start | bytes 91400 | tf_op jit(solution)/shard_map/ppermute | solution.py:25
Sparse Core Ops, SparseCore 0:
  14.1 253.6 all-reduce.1
where the time goes:
time: 366 us; the launch traced here: 365 us
  waiting for transfers between devices  283 us (77%)
  starting transfers between devices  31 us (8%)
  other arithmetic  24.9 us (7%)
  between operations  14.4 us (4%)
  matrix products  10.9 us (3%)
    psum x1, waiting for transfers between devices, body(): total = lax.psum(local, ('wide', 'narrow'))  258 us
    ppermute x6, waiting for transfers between devices, with_halo(): lax.ppermute(head, axis, [((i + 1) % count, i) for i in range(ends)])  24.4 us
    ppermute x6, starting transfers between devices, with_halo(): lax.ppermute(tail, axis, [(i, (i + 1) % count) for i in range(ends)])  15.9 us
    ppermute x6, starting transfers between devices, with_halo(): lax.ppermute(head, axis, [((i + 1) % count, i) for i in range(ends)])  15.1 us
    another operation x12, other arithmetic, subspace(): lower = jnp.linalg.cholesky(inner)  8.57 us
    another operation x8, other arithmetic, subspace(): basis = jax.scipy.linalg.solve_triangular(lower, grown.T, lower=True).T  7.51 us
  transfers between devices with their start and end apart: 13, of which 7 were waited for; matrix products, arithmetic and copies ran while one was open for 0% of the time, Pallas kernels for 0%

commit v1 on v0

--- a/solution.py
+++ b/solution.py
@@ -10,6 +10,12 @@
 POWER_ITERS = 4
 TV_ITERS = 3
 hi_prec = lax.Precision.HIGHEST
+
+
+def summed_here(block, axis):
+    pieces = lax.all_gather(block, axis, axis=0, tiled=False)
+    result = pieces.sum(axis=0)
+    return result
 
 
 def with_halo(cells, sides, width):
@@ -71,7 +77,7 @@
     local = lax.dot_general(
         flat, flat, (((0,), (0,)), ((), ())), preferred_element_type=jnp.float32
     )
-    total = lax.psum(local, ("wide", "narrow"))
+    total = summed_here(local, ("wide", "narrow"))
     gram = total / (height * width)
     basis = subspace(gram)
     projector = jnp.dot(basis, basis.T, precision=hi_prec)

time: 366 us -> 324 us (0.89)
  waiting for transfers between devices: 283 us -> 224 us
  other arithmetic: 24.9 us -> 43.8 us
  matrix products: 10.9 us -> 7.14 us
    psum x1 -> x0, waiting for transfers between devices: 258 us -> none  [body(): total = lax.psum(local, ('wide', 'narrow'))]
    all_gather x0 -> x1, waiting for transfers between devices: none -> 199 us  [summed_here(): pieces = lax.all_gather(block, axis, axis=0, tiled=False)]
    reduce_sum x0 -> x1, other arithmetic: none -> 18.6 us  [summed_here(): result = pieces.sum(axis=0)]
    dot_general x4, matrix products: 5.3 us -> 1.54 us  [subspace(): grown = jnp.dot(gram, basis, precision=hi_prec)]
  transfers between devices with their start and end apart: 13 -> 13, of which waited for: 7 -> 7; matrix products, arithmetic and copies ran while one was open for 0% -> 1% of each run, Pallas kernels for 0% -> 0%
where the time goes in v1:
time: 324 us; the launch traced here: 323 us
  waiting for transfers between devices  224 us (69%)
  other arithmetic  43.8 us (14%)
  starting transfers between devices  32.6 us (10%)
  between operations  14.4 us (4%)
  matrix products  7.14 us (2%)
    all_gather x1, waiting for transfers between devices, summed_here(): pieces = lax.all_gather(block, axis, axis=0, tiled=False)  199 us
    ppermute x6, waiting for transfers between devices, with_halo(): lax.ppermute(head, axis, [((i + 1) % count, i) for i in range(ends)])  24.9 us
    reduce_sum x1, other arithmetic, summed_here(): result = pieces.sum(axis=0)  18.6 us
    ppermute x6, starting transfers between devices, with_halo(): lax.ppermute(tail, axis, [(i, (i + 1) % count) for i in range(ends)])  18 us
    ppermute x6, starting transfers between devices, with_halo(): lax.ppermute(head, axis, [((i + 1) % count, i) for i in range(ends)])  14.6 us
    another operation x12, other arithmetic, subspace(): lower = jnp.linalg.cholesky(inner)  8.57 us
    another operation x8, other arithmetic, subspace(): basis = jax.scipy.linalg.solve_triangular(lower, grown.T, lower=True).T  7.51 us
  transfers between devices with their start and end apart: 13, of which 7 were waited for; matrix products, arithmetic and copies ran while one was open for 1% of the time, Pallas kernels for 0%

profile of v1, /device:TPU:111, one launch (start us, length us, event | category | flops | bytes accessed | tf_op | source)
XLA Modules:
  0.0 323.1 jit_solution(309271315938001995)
XLA Ops:
  7.2 1.1 copy-done
  8.3 1.1 convolution_bitcast_fusion.1
  9.5 198.8 %all-gather.3.cloned.1.call-done = f32[57344,224]{1,0:T(8,128)} async-done(((f32[224,224]{1,0:T(8,128)}), f32[57344,224]{1,0:T(8,128)}) %all-gather.3.cloned.1.call-update) | async-done | bytes 51380240 | tf_op jit(solution)/shard_map/all_gather | solution.py:16
  208.3 18.6 %reduce_sum.9 = f32[224,224]{1,0:T(8,128)S(1)} reduce(f32[256,224,224]{2,1,0:T(8,128)} %bitcast.76, f32[]{:T(128)} %constant.58.clone.1), dimensions={0}, to_apply=%region_0.0 | reduce | flops 12794880 | bytes 51580932 | tf_op jit(solution)/shard_map/reduce_sum | solution.py:17
  226.9 0.7 fusion.34
  227.9 1.5 cholesky.74
  229.4 0.6 compare_reduce_fusion.3
  230.0 0.6 fusion.56
  230.7 1.2 custom-call.8
  232.7 1.5 cholesky.85
  234.2 0.6 compare_reduce_fusion.2
  234.8 0.6 fusion.57
  235.5 1.2 custom-call.9
  237.5 1.5 cholesky.96
  238.9 0.6 compare_reduce_fusion.1
  239.6 0.6 fusion.58
  240.3 1.2 custom-call.10
  242.2 1.5 cholesky.107
  243.7 0.6 compare_reduce_fusion
  244.4 0.6 fusion.59
  245.0 1.2 custom-call.11
  246.5 0.5 convolution_bitcast_fusion
  246.9 1.5 fusion.46
  248.4 3.0 collective-permute-start
  251.5 1.9 collective-permute-start.1
  253.4 3.5 %collective-permute-done.1 = f32[1,48,224]{2,1,0:T(8,128)S(1)} collective-permute-done((f32[1,48,224]{2,1,0:T(8,128)S(1)}, f32[1,48,224]{2,1,0:T(8,128)S(1)}, u32[]{:S(2)}, u32[]{:S(2)}) %collective-permute-start.1) | collective-permute-done | bytes 43040 | tf_op jit(solution)/shard_map/ppermute | solution.py:31
  257.0 4.1 %collective-permute-start.2 = (f32[34,1,224]{2,1,0:T(1,128)S(1)}, f32[34,1,224]{2,1,0:T(1,128)S(1)}, u32[]{:S(2)}, u32[]{:S(2)}) collective-permute-start(f32[34,1,224]{2,1,0:T(1,128)S(1)} %get-tuple-element.15), channel_id=1, source_target_pairs={{0,8},{8,16},{16,24},{24,32},{32,40},{40,48},{48,56},{56,64},{64,7... | collective-permute-start | bytes 91400 | tf_op jit(solution)/shard_map/ppermute | solution.py:29
  261.1 1.9 collective-permute-start.3
  263.2 5.9 %collective-permute-done.3 = f32[34,1,224]{2,1,0:T(1,128)S(1)} collective-permute-done((f32[34,1,224]{2,1,0:T(1,128)S(1)}, f32[34,1,224]{2,1,0:T(1,128)S(1)}, u32[]{:S(2)}, u32[]{:S(2)}) %collective-permute-start.3) | collective-permute-done | bytes 30496 | tf_op jit(solution)/shard_map/ppermute | solution.py:31
  269.1 1.4 fusion.14
  270.5 0.9 fusion.27
  271.4 3.6 %collective-permute-start.4 = (f32[1,48,224]{2,1,0:T(8,128)S(1)}, f32[1,48,224]{2,1,0:T(8,128)S(1)}, u32[]{:S(2)}, u32[]{:S(2)}) collective-permute-start(f32[1,48,224]{2,1,0:T(8,128)S(1)} %get-tuple-element.18), channel_id=1, source_target_pairs={{0,1},{1,2},{2,3},{3,4},{4,5},{5,6},{6,7},{8,9},{9,10},{10,11},{11... | collective-permute-start | bytes 129032 | tf_op jit(solution)/shard_map/ppermute | solution.py:29
  275.1 1.9 collective-permute-start.5
  277.0 3.5 %collective-permute-done.5 = f32[1,48,224]{2,1,0:T(8,128)S(1)} collective-permute-done((f32[1,48,224]{2,1,0:T(8,128)S(1)}, f32[1,48,224]{2,1,0:T(8,128)S(1)}, u32[]{:S(2)}, u32[]{:S(2)}) %collective-permute-start.5) | collective-permute-done | bytes 43040 | tf_op jit(solution)/shard_map/ppermute | solution.py:31
  280.5 1.9 collective-permute-start.6
  282.5 3.4 %collective-permute-start.7 = (f32[34,1,224]{2,1,0:T(1,128)S(1)}, f32[34,1,224]{2,1,0:T(1,128)S(1)}, u32[]{:S(2)}, u32[]{:S(2)}) collective-permute-start(f32[34,1,224]{2,1,0:T(1,128)S(1)} %get-tuple-element.12), channel_id=1, source_target_pairs={{8,0},{16,8},{24,16},{32,24},{40,32},{48,40},{56,48},{64,56},{72,6... | collective-permute-start | bytes 91400 | tf_op jit(solution)/shard_map/ppermute | solution.py:31
  286.1 4.4 %collective-permute-done.7 = f32[34,1,224]{2,1,0:T(1,128)S(1)} collective-permute-done((f32[34,1,224]{2,1,0:T(1,128)S(1)}, f32[34,1,224]{2,1,0:T(1,128)S(1)}, u32[]{:S(2)}, u32[]{:S(2)}) %collective-permute-start.7) | collective-permute-done | bytes 30496 | tf_op jit(solution)/shard_map/ppermute | solution.py:31
  290.5 1.4 fusion.12
  291.9 1.1 fusion.23
  293.0 3.4 %collective-permute-start.8 = (f32[1,48,224]{2,1,0:T(8,128)S(1)}, f32[1,48,224]{2,1,0:T(8,128)S(1)}, u32[]{:S(2)}, u32[]{:S(2)}) collective-permute-start(f32[1,48,224]{2,1,0:T(8,128)S(1)} %get-tuple-element.16), channel_id=1, source_target_pairs={{0,1},{1,2},{2,3},{3,4},{4,5},{5,6},{6,7},{8,9},{9,10},{10,11},{11... | collective-permute-start | bytes 129032 | tf_op jit(solution)/shard_map/ppermute | solution.py:29
  296.3 1.9 collective-permute-start.9
  298.3 3.5 %collective-permute-done.9 = f32[1,48,224]{2,1,0:T(8,128)S(1)} collective-permute-done((f32[1,48,224]{2,1,0:T(8,128)S(1)}, f32[1,48,224]{2,1,0:T(8,128)S(1)}, u32[]{:S(2)}, u32[]{:S(2)}) %collective-permute-start.9) | collective-permute-done | bytes 43040 | tf_op jit(solution)/shard_map/ppermute | solution.py:31
  301.8 1.9 collective-permute-start.10
  303.7 1.1 fusion.88
  304.8 3.5 %collective-permute-start.11 = (f32[34,1,224]{2,1,0:T(1,128)S(1)}, f32[34,1,224]{2,1,0:T(1,128)S(1)}, u32[]{:S(2)}, u32[]{:S(2)}) collective-permute-start(f32[34,1,224]{2,1,0:T(1,128)S(1)} %get-tuple-element.10), channel_id=1, source_target_pairs={{8,0},{16,8},{24,16},{32,24},{40,32},{48,40},{56,48},{64,56},{72,6... | collective-permute-start | bytes 91400 | tf_op jit(solution)/shard_map/ppermute | solution.py:31
  308.5 4.2 %collective-permute-done.11 = f32[34,1,224]{2,1,0:T(1,128)S(1)} collective-permute-done((f32[34,1,224]{2,1,0:T(1,128)S(1)}, f32[34,1,224]{2,1,0:T(1,128)S(1)}, u32[]{:S(2)}, u32[]{:S(2)}) %collective-permute-start.11) | collective-permute-done | bytes 30496 | tf_op jit(solution)/shard_map/ppermute | solution.py:31
  312.8 1.4 fusion.10
  314.2 2.0 fusion.19
  (48 shorter events, 3.7 us)
Async XLA Ops:
  7.2 1.1 copy-start
  7.2 201.1 %all-gather.3.cloned.1.call-start = ((), (), s32[]{:S(2)}) async-start(), calls=%async_computation | async-start | bytes 58949632 | tf_op jit(solution)/shard_map/all_gather | solution.py:16
  248.4 5.0 %collective-permute-start = (f32[1,48,224]{2,1,0:T(8,128)S(1)}, f32[1,48,224]{2,1,0:T(8,128)S(1)}, u32[]{:S(2)}, u32[]{:S(2)}) collective-permute-start(f32[1,48,224]{2,1,0:T(8,128)S(1)} %get-tuple-element.20), channel_id=1, source_target_pairs={{0,1},{1,2},{2,3},{3,4},{4,5},{5,6},{6,7},{8,9},{9,10},{10,11},{11... | collective-permute-start | bytes 129032 | tf_op jit(solution)/shard_map/ppermute | solution.py:29
  251.5 5.4 %collective-permute-start.1 = (f32[1,48,224]{2,1,0:T(8,128)S(1)}, f32[1,48,224]{2,1,0:T(8,128)S(1)}, u32[]{:S(2)}, u32[]{:S(2)}) collective-permute-start(f32[1,48,224]{2,1,0:T(8,128)S(1)} %get-tuple-element.21), channel_id=1, source_target_pairs={{1,0},{2,1},{3,2},{4,3},{5,4},{6,5},{7,6},{9,8},{10,9},{11,10},{12... | collective-permute-start | bytes 129032 | tf_op jit(solution)/shard_map/ppermute | solution.py:31
  257.0 6.1 %collective-permute-start.2 = (f32[34,1,224]{2,1,0:T(1,128)S(1)}, f32[34,1,224]{2,1,0:T(1,128)S(1)}, u32[]{:S(2)}, u32[]{:S(2)}) collective-permute-start(f32[34,1,224]{2,1,0:T(1,128)S(1)} %get-tuple-element.15), channel_id=1, source_target_pairs={{0,8},{8,16},{16,24},{24,32},{32,40},{40,48},{48,56},{56,64},{64,7... | collective-permute-start | bytes 91400 | tf_op jit(solution)/shard_map/ppermute | solution.py:29
  261.1 8.0 %collective-permute-start.3 = (f32[34,1,224]{2,1,0:T(1,128)S(1)}, f32[34,1,224]{2,1,0:T(1,128)S(1)}, u32[]{:S(2)}, u32[]{:S(2)}) collective-permute-start(f32[34,1,224]{2,1,0:T(1,128)S(1)} %get-tuple-element.14), channel_id=1, source_target_pairs={{8,0},{16,8},{24,16},{32,24},{40,32},{48,40},{56,48},{64,56},{72,6... | collective-permute-start | bytes 91400 | tf_op jit(solution)/shard_map/ppermute | solution.py:31
  271.4 5.6 %collective-permute-start.4 = (f32[1,48,224]{2,1,0:T(8,128)S(1)}, f32[1,48,224]{2,1,0:T(8,128)S(1)}, u32[]{:S(2)}, u32[]{:S(2)}) collective-permute-start(f32[1,48,224]{2,1,0:T(8,128)S(1)} %get-tuple-element.18), channel_id=1, source_target_pairs={{0,1},{1,2},{2,3},{3,4},{4,5},{5,6},{6,7},{8,9},{9,10},{10,11},{11... | collective-permute-start | bytes 129032 | tf_op jit(solution)/shard_map/ppermute | solution.py:29
  275.1 5.4 %collective-permute-start.5 = (f32[1,48,224]{2,1,0:T(8,128)S(1)}, f32[1,48,224]{2,1,0:T(8,128)S(1)}, u32[]{:S(2)}, u32[]{:S(2)}) collective-permute-start(f32[1,48,224]{2,1,0:T(8,128)S(1)} %get-tuple-element.19), channel_id=1, source_target_pairs={{1,0},{2,1},{3,2},{4,3},{5,4},{6,5},{7,6},{9,8},{10,9},{11,10},{12... | collective-permute-start | bytes 129032 | tf_op jit(solution)/shard_map/ppermute | solution.py:31
  280.5 5.3 %collective-permute-start.6 = (f32[34,1,224]{2,1,0:T(1,128)S(1)}, f32[34,1,224]{2,1,0:T(1,128)S(1)}, u32[]{:S(2)}, u32[]{:S(2)}) collective-permute-start(f32[34,1,224]{2,1,0:T(1,128)S(1)} %get-tuple-element.13), channel_id=1, source_target_pairs={{0,8},{8,16},{16,24},{24,32},{32,40},{40,48},{48,56},{56,64},{64,7... | collective-permute-start | bytes 91400 | tf_op jit(solution)/shard_map/ppermute | solution.py:29
  282.5 8.0 %collective-permute-start.7 = (f32[34,1,224]{2,1,0:T(1,128)S(1)}, f32[34,1,224]{2,1,0:T(1,128)S(1)}, u32[]{:S(2)}, u32[]{:S(2)}) collective-permute-start(f32[34,1,224]{2,1,0:T(1,128)S(1)} %get-tuple-element.12), channel_id=1, source_target_pairs={{8,0},{16,8},{24,16},{32,24},{40,32},{48,40},{56,48},{64,56},{72,6... | collective-permute-start | bytes 91400 | tf_op jit(solution)/shard_map/ppermute | solution.py:31
  293.0 5.3 %collective-permute-start.8 = (f32[1,48,224]{2,1,0:T(8,128)S(1)}, f32[1,48,224]{2,1,0:T(8,128)S(1)}, u32[]{:S(2)}, u32[]{:S(2)}) collective-permute-start(f32[1,48,224]{2,1,0:T(8,128)S(1)} %get-tuple-element.16), channel_id=1, source_target_pairs={{0,1},{1,2},{2,3},{3,4},{4,5},{5,6},{6,7},{8,9},{9,10},{10,11},{11... | collective-permute-start | bytes 129032 | tf_op jit(solution)/shard_map/ppermute | solution.py:29
  296.3 5.4 %collective-permute-start.9 = (f32[1,48,224]{2,1,0:T(8,128)S(1)}, f32[1,48,224]{2,1,0:T(8,128)S(1)}, u32[]{:S(2)}, u32[]{:S(2)}) collective-permute-start(f32[1,48,224]{2,1,0:T(8,128)S(1)} %get-tuple-element.17), channel_id=1, source_target_pairs={{1,0},{2,1},{3,2},{4,3},{5,4},{6,5},{7,6},{9,8},{10,9},{11,10},{12... | collective-permute-start | bytes 129032 | tf_op jit(solution)/shard_map/ppermute | solution.py:31
  301.8 6.5 %collective-permute-start.10 = (f32[34,1,224]{2,1,0:T(1,128)S(1)}, f32[34,1,224]{2,1,0:T(1,128)S(1)}, u32[]{:S(2)}, u32[]{:S(2)}) collective-permute-start(f32[34,1,224]{2,1,0:T(1,128)S(1)} %get-tuple-element.11), channel_id=1, source_target_pairs={{0,8},{8,16},{16,24},{24,32},{32,40},{40,48},{48,56},{56,64},{64,7... | collective-permute-start | bytes 91400 | tf_op jit(solution)/shard_map/ppermute | solution.py:29
  304.8 8.0 %collective-permute-start.11 = (f32[34,1,224]{2,1,0:T(1,128)S(1)}, f32[34,1,224]{2,1,0:T(1,128)S(1)}, u32[]{:S(2)}, u32[]{:S(2)}) collective-permute-start(f32[34,1,224]{2,1,0:T(1,128)S(1)} %get-tuple-element.10), channel_id=1, source_target_pairs={{8,0},{16,8},{24,16},{32,24},{40,32},{48,40},{56,48},{64,56},{72,6... | collective-permute-start | bytes 91400 | tf_op jit(solution)/shard_map/ppermute | solution.py:31
  314.2 2.0 copy-start.1
Sparse Core Ops, SparseCore 0:
  12.1 196.1 all-gather.2
